TPU v7x, 32 devices: a whole 2x2x4 slice. The times are simulated.
32 devices in a mesh: subset: 2 (over core), slab: 16 (over z, y, x).
Axes of the slice: x: 2, y: 2, z: 4, core: 2. Of those that a mesh axis runs over, the one named last changes fastest.
Arguments:
- z_field: float32 [1, 2048, 2048], P(None, 'slab'), may hold values from -6 to 6
- duals: float32 [2, 1, 2048, 2048], P('subset', None, 'slab'), may hold values from -3 to 3
- tiles: bfloat16 [2, 128, 128, 128], P('subset', 'slab'), may hold values from -0.1875 to 0.1875
- ray_index: int32 [2, 128], P('subset', 'slab'), may hold values from 0 to 15
- pixel_index: int32 [2, 128], P('subset', 'slab'), may hold values from 0 to 2047, as said below
- measured: float32 [2, 1, 2048], P('subset'), may hold values from -6 to 6
- step_size: float32 [2], P('subset'), may hold values from 0.2 to 0.6
- kernel: float32 [3, 3, 3], replicated, may hold values from -0.6 to 0.6
Outputs:
- new_field: float32 [1, 2048, 2048], P(None, 'slab')
- new_duals: float32 [2, 1, 2048, 2048], P('subset', None, 'slab')
Inputs may be any that keep to these rules, and one draw needn't show every extreme that they name: `pixel_index`: for each subset and each slab owner, the 8 tiles of the owner name 8 different pixel blocks of its slab.
All inputs are finite; a program needn't handle non-finite values.
Results may differ from a plain program's by a relative error of at most 0.0028.
Values may be sent and summed in bfloat16 or wider, within the bound.
A program may use at most 128 MiB of HBM per device.

v0:
```python
import math

import jax
import jax.numpy as jnp
from jax import lax
from jax.sharding import PartitionSpec as P


def extended(value, sides, width):
    for axis, dim in sides:
        count, length = (lax.axis_size(axis), value.shape[dim])
        up = [(i, (i + 1) % count) for i in range(count - 1)]
        down = [(j, i) for i, j in up]
        last = lax.slice_in_dim(value, length - width, length, axis=dim)
        first = lax.slice_in_dim(value, 0, width, axis=dim)
        before = lax.ppermute(last, axis, up)
        after = lax.ppermute(first, axis, down)
        value = jnp.concatenate([before, value, after], axis=dim)
    return value


def body(z_field, duals, tiles, ray_index, pixel_index, measured, step_size, kernel):
    slice_count, row_count, width_count = z_field.shape
    dual_part = duals[0]
    tile_values = tiles[0]
    block_size = tile_values.shape[1]
    ray_count = measured.shape[2]
    ray_blocks = ray_count // block_size
    pixel_blocks = row_count * width_count // block_size
    ray_ids = ray_index[0]
    pixel_ids = pixel_index[0]
    start_field = z_field - dual_part
    flat_blocks = start_field.astype(jnp.bfloat16).reshape(slice_count, pixel_blocks, block_size)
    chosen_blocks = jnp.take(flat_blocks, pixel_ids, axis=1)
    contrib = jnp.einsum(
        "snp,nrp->snr", chosen_blocks, tile_values, preferred_element_type=jnp.float32
    )
    ray_onehot = (ray_ids[:, None] == jnp.arange(ray_blocks, dtype=jnp.int32)[None, :]).astype(
        jnp.float32
    )
    partial_rays = jnp.einsum(
        "snr,nk->skr", contrib, ray_onehot, precision=lax.Precision.HIGHEST
    ).reshape(slice_count, ray_count)
    target = measured[0]
    total_rays = lax.psum(partial_rays, "slab")
    residual = (total_rays - target).astype(jnp.bfloat16)
    picked_rays = jnp.take(residual.reshape(slice_count, ray_blocks, block_size), ray_ids, axis=1)
    back_terms = jnp.einsum(
        "snr,nrp->snp", picked_rays, tile_values, preferred_element_type=jnp.float32
    )
    pixel_onehot = (
        pixel_ids[:, None] == jnp.arange(pixel_blocks, dtype=jnp.int32)[None, :]
    ).astype(jnp.float32)
    back_sum = jnp.einsum(
        "snp,nk->skp", back_terms, pixel_onehot, precision=lax.Precision.HIGHEST
    ).reshape(slice_count, row_count, width_count)
    estimate = start_field - step_size[0] * (width_count / math.sqrt(ray_count)) * back_sum
    average = lax.psum(estimate + dual_part, "subset") / lax.axis_size("subset")
    bordered = extended(average, (("slab", 1),), 1)
    bordered = jnp.pad(bordered, ((1, 1), (0, 0), (0, 0)))
    zero_column = jnp.zeros((slice_count + 2, row_count + 2, 1), jnp.float32)
    left_cells = jnp.concatenate([zero_column, bordered[:, :, :-1]], axis=2)
    right_cells = jnp.concatenate([bordered[:, :, 1:], zero_column], axis=2)
    column_stack = jnp.stack([left_cells, bordered, right_cells], axis=0)
    row_stack = jnp.stack(
        [column_stack[:, :, offset_b : offset_b + row_count] for offset_b in range(3)], axis=0
    )
    full_stack = jnp.stack(
        [row_stack[:, :, offset_a : offset_a + slice_count] for offset_a in range(3)], axis=0
    )
    filtered = jnp.einsum("abc,abcsrw->srw", kernel, full_stack, precision=lax.Precision.HIGHEST)
    new_field = average + filtered
    new_duals = dual_part + estimate - new_field
    return (new_field, new_duals[None])


def solution(mesh):
    placed = (
        P(None, "slab", None),
        P("subset", None, "slab", None),
        P("subset", "slab", None, None),
        P("subset", "slab"),
        P("subset", "slab"),
        P("subset", None, None),
        P("subset"),
        P(),
    )
    return jax.shard_map(
        body,
        mesh=mesh,
        in_specs=placed,
        out_specs=(P(None, "slab", None), P("subset", None, "slab", None)),
        check_vma=False,
    )
```

profile of v0, /device:TPU:0, one launch (start us, length us, event | category | flops | bytes accessed | tf_op | source)
XLA Modules:
  0.0 242.5 jit_solution(17154660392934144605)
XLA Ops:
  7.2 0.7 compare_and_fusion.1
  7.9 0.7 fusion.17
  8.6 0.7 compare_and_fusion
  10.6 1.7 fusion.3
  13.4 0.9 fusion.14
  14.3 44.0 %psum.14 = f32[1,2048]{1,0:T(1,128)S(1)} all-reduce(f32[1,2048]{1,0:T(1,128)S(1)} %bitcast.77), channel_id=1, replica_groups=mesh['subset'=2,'slab'=16] {'slab'}, use_global_device_ids=true, to_apply=%region_0.1 | all-reduce | flops 2048 | bytes 16384 | tf_op jit(solution)/shard_map/psum | solution.py:45
  58.3 0.7 fusion.10
  59.9 1.7 convolution_multiply_fusion
  61.8 2.7 %bitcast_add_fusion.1 = f32[1,128,2048]{2,1,0:T(8,128)} fusion(f32[1,1,128,2048]{3,2,1,0:T(8,128)} %param.9, f32[1,128,2048]{2,1,0:T(8,128)S(1)} %mul.27, f32[1,128,2048]{2,1,0:T(8,128)} %param.8), kind=kLoop, calls=%fused_computation.22 | loop fusion | flops 786432 | bytes 4194304 | tf_op jit(solution)/shard_map/add | solution.py:58
  64.5 15.4 %all-reduce.5.cloned.1.call-done = f32[1,128,2048]{2,1,0:T(8,128)} async-done(((f32[1,128,2048]{2,1,0:T(8,128)}), f32[1,128,2048]{2,1,0:T(8,128)}) %all-reduce.5.cloned.1.call-update) | async-done | bytes 1048592 | tf_op jit(solution)/shard_map/psum | solution.py:58
  79.9 1.3 broadcast_multiply_fusion
  81.3 3.7 %collective-permute-start = (f32[1,1,2048]{2,1,0:T(1,128)S(1)}, f32[1,1,2048]{2,1,0:T(1,128)S(1)}, u32[]{:S(2)}, u32[]{:S(2)}) collective-permute-start(f32[1,1,2048]{2,1,0:T(1,128)S(1)} %get-tuple-element.14), channel_id=1, source_target_pairs={{0,1},{1,2},{2,3},{3,4},{4,5},{5,6},{6,7},{7,8},{8,9},{9,10},{10,1... | collective-permute-start | bytes 24584 | tf_op jit(solution)/shard_map/ppermute | solution.py:16
  84.9 1.3 collective-permute-start.1
  86.3 4.2 %collective-permute-done.1 = f32[1,1,2048]{2,1,0:T(1,128)S(1)} collective-permute-done((f32[1,1,2048]{2,1,0:T(1,128)S(1)}, f32[1,1,2048]{2,1,0:T(1,128)S(1)}, u32[]{:S(2)}, u32[]{:S(2)}) %collective-permute-start.1) | collective-permute-done | bytes 8224 | tf_op jit(solution)/shard_map/ppermute | solution.py:17
  90.5 2.1 fusion.18
  92.6 1.3 fusion.19
  94.0 3.1 %pad_bitcast_fusion = (f32[1,3,130,2048]{3,2,1,0:T(8,128)S(1)}, f32[1,3,130,2048]{3,2,1,0:T(8,128)}) fusion(f32[3,130,2047]{2,1,0:T(8,128)S(1)} %get-tuple-element.11, f32[3,130,2047]{2,1,0:T(8,128)S(1)} %get-tuple-element.10), kind=kLoop, calls=%fused_computation.17 | loop fusion | bytes 12776400 | tf_op jit(solution)/shard_map/stack | solution.py:64
  97.1 4.4 %pad_maximum_fusion.1 = f32[3,3,130,2048]{3,2,1,0:T(8,128)S(1)} fusion(f32[1,3,130,2048]{3,2,1,0:T(8,128)S(1)} %get-tuple-element.16, f32[1,3,130,2048]{3,2,1,0:T(8,128)} %get-tuple-element.12, f32[1,3,130,2048]{3,2,1,0:T(8,128)} %get-tuple-element.17), kind=kLoop, calls=%fused_computation.6 | loop fusion | flops 4792320 | bytes 19169280 | tf_op jit(solution)/shard_map/stack | solution.py:64
  101.5 10.0 %slice_bitcast_fusion.5 = (f32[1,3,3,128,2048]{4,3,2,1,0:T(8,128)}, f32[1,3,3,128,2048]{4,3,2,1,0:T(8,128)}, f32[1,3,3,128,2048]{4,3,2,1,0:T(8,128)}) fusion(f32[3,3,130,2048]{3,2,1,0:T(8,128)S(1)} %pad_maximum_fusion.1), kind=kLoop, calls=%fused_computation.12 | loop fusion | bytes 56623104 | tf_op jit(solution)/shard_map/stack | solution.py:65
  111.4 20.5 %pad_maximum_fusion = f32[3,3,3,128,2048]{4,3,2,1,0:T(8,128)} fusion(f32[1,3,3,128,2048]{4,3,2,1,0:T(8,128)} %get-tuple-element.8, f32[1,3,3,128,2048]{4,3,2,1,0:T(8,128)} %get-tuple-element.9, f32[1,3,3,128,2048]{4,3,2,1,0:T(8,128)} %get-tuple-element.7), kind=kLoop, calls=%fused_computation.4 | loop fusion | flops 14155776 | bytes 56623104 | tf_op jit(solution)/shard_map/stack | solution.py:65
  131.9 14.3 %slice_bitcast_fusion.2 = (f32[1,3,3,1,128,2048]{5,4,2,1,3,0:T(8,128)S(1)}, f32[1,3,3,1,128,2048]{5,4,2,1,3,0:T(8,128)S(1)}, f32[1,3,3,1,128,2048]{5,4,2,1,3,0:T(8,128)}) fusion(f32[3,3,3,128,2048]{4,3,2,1,0:T(8,128)} %pad_maximum_fusion), kind=kLoop, calls=%fused_computation.9 | loop fusion | bytes 56623104 | tf_op jit(solution)/shard_map/stack | solution.py:68
  146.2 13.2 %maximum_bitcast_fusion = f32[3,3,3,128,2048]{4,3,2,1,0:T(8,128)} fusion(f32[1,3,3,1,128,2048]{5,4,2,1,3,0:T(8,128)S(1)} %get-tuple-element.5, f32[1,3,3,1,128,2048]{5,4,2,1,3,0:T(8,128)} %get-tuple-element.6, f32[1,3,3,1,128,2048]{5,4,2,1,3,0:T(8,128)S(1)} %get-tuple-element.4), kind=kLoop, calls=%fused_computation.5 | loop fusion | flops 14155776 | bytes 56623104 | tf_op jit(solution)/shard_map/reshape.18
  159.4 74.3 %fusion = f32[1,128,2048,1,1]{2,0,4,3,1:T(1,128)S(1)} fusion(f32[3,3,3,128,2048]{4,3,2,1,0:T(8,128)} %maximum_bitcast_fusion, f32[3,3,3,1,1]{2,1,0,3,4:T(4,128)S(1)} %bitcast.79), kind=kOutput, calls=%fused_computation.2 | convolution fusion | flops 84934656 | bytes 29360236 | tf_op jit(solution)/shard_map/abc,abcsrw->srw/dot_general | solution.py:71
  233.8 1.9 subtract_bitcast_fusion
  (25 shorter events, 2.9 us)
Async XLA Ops:
  7.2 6.0 %copy-start = (bf16[1,8,128,128]{3,2,1,0:T(8,128)(2,1)S(1)}, bf16[1,8,128,128]{3,2,1,0:T(8,128)(2,1)}, u32[]{:S(2)}) copy-start(bf16[1,8,128,128]{3,2,1,0:T(8,128)(2,1)} %param.10) | copy-start | bytes 786436
  7.2 72.7 %all-reduce.5.cloned.1.call-start = ((), (), s32[]{:S(2)}) async-start(), calls=%async_computation | async-start | bytes 2097152 | tf_op jit(solution)/shard_map/psum | solution.py:58
  81.3 5.0 %collective-permute-start = (f32[1,1,2048]{2,1,0:T(1,128)S(1)}, f32[1,1,2048]{2,1,0:T(1,128)S(1)}, u32[]{:S(2)}, u32[]{:S(2)}) collective-permute-start(f32[1,1,2048]{2,1,0:T(1,128)S(1)} %get-tuple-element.14), channel_id=1, source_target_pairs={{0,1},{1,2},{2,3},{3,4},{4,5},{5,6},{6,7},{7,8},{8,9},{9,10},{10,1... | collective-permute-start | bytes 24584 | tf_op jit(solution)/shard_map/ppermute | solution.py:16
  84.9 5.5 %collective-permute-start.1 = (f32[1,1,2048]{2,1,0:T(1,128)S(1)}, f32[1,1,2048]{2,1,0:T(1,128)S(1)}, u32[]{:S(2)}, u32[]{:S(2)}) collective-permute-start(f32[1,1,2048]{2,1,0:T(1,128)S(1)} %get-tuple-element.15), channel_id=1, source_target_pairs={{1,0},{2,1},{3,2},{4,3},{5,4},{6,5},{7,6},{8,7},{9,8},{10,9},{11,1... | collective-permute-start | bytes 24584 | tf_op jit(solution)/shard_map/ppermute | solution.py:17
  146.2 13.2 %copy-start.4 = (f32[3,3,3]{2,1,0:T(4,128)S(1)}, f32[3,3,3]{2,1,0:T(4,128)}, u32[]{:S(2)}) copy-start(f32[3,3,3]{2,1,0:T(4,128)} %param.15) | copy-start | bytes 328
  159.4 74.4 %copy-start.2 = (f32[1,128,2048]{2,1,0:T(8,128)S(1)}, f32[1,128,2048]{2,1,0:T(8,128)}, u32[]{:S(2)}) copy-start(f32[1,128,2048]{2,1,0:T(8,128)} %bitcast_add_fusion.1) | copy-start | bytes 3145732
  159.4 74.4 %copy-start.3 = (f32[1,128,2048]{2,1,0:T(8,128)S(1)}, f32[1,128,2048]{2,1,0:T(8,128)}, u32[]{:S(2)}) copy-start(f32[1,128,2048]{2,1,0:T(8,128)} %all-reduce.5.cloned.1.call-done) | copy-start | bytes 3145732
  159.4 76.3 %copy-start.1 = (bf16[1,8,128,128]{3,2,1,0:T(8,128)(2,1)S(1)}, bf16[1,8,128,128]{3,2,1,0:T(8,128)(2,1)}, u32[]{:S(2)}) copy-start(bf16[1,8,128,128]{3,2,1,0:T(8,128)(2,1)} %param.10) | copy-start | bytes 786436
Sparse Core Ops, SparseCore 0:
  64.6 15.2 all-reduce.4
where the time goes:
time: 243 us
  matrix products  77.4 us (32%)
  other arithmetic  51.3 us (21%)
  blocking collectives  44 us (18%)
  local copies, waits for them, and re-layouts  30.3 us (12%)
  waiting for transfers between devices  19.7 us (8%)
  between operations  14.8 us (6%)
  starting transfers between devices  4.99 us (2%)
    dot_general x1, matrix products, body(): jnp.einsum('abc,abcsrw->srw', kernel, full_stack, precision=lax.Precision...  74.3 us
    psum x1, blocking collectives, body(): total_rays = lax.psum(partial_rays, 'slab')  44 us
    another operation x1, other arithmetic, body(): jnp.stack([column_stack[:, :, offset_b:offset_b + row_count] for offset_b...  20.5 us
    psum x1, waiting for transfers between devices, body(): average = lax.psum(estimate + dual_part, 'subset') / lax.axis_size('subset')  15.4 us
    another operation x1, local copies, waits for them, and re-layouts, body(): jnp.stack([row_stack[:, :, offset_a:offset_a + slice_count] for offset_a...  14.3 us
    another operation x1, other arithmetic  13.2 us
    another operation x1, local copies, waits for them, and re-layouts, body(): jnp.stack([column_stack[:, :, offset_b:offset_b + row_count] for offset_b...  9.97 us
    another operation x2, other arithmetic, body(): column_stack = jnp.stack([left_cells, bordered, right_cells], axis=0)  6.5 us
  transfers between devices with their start and end apart: 3, of which 2 were waited for; matrix products, arithmetic and copies ran while one was open for 0% of the time, Pallas kernels for 0%

commit v1 on v0

v1 whole, which is shorter than its diff:
```python
import functools
import math

import jax
import jax.numpy as jnp
from jax import lax
from jax.experimental import pallas as pl
from jax.experimental.pallas import tpu as pltpu
from jax.sharding import PartitionSpec as P

MESH = pl.DeviceIdType.MESH


def split_group(count):
    inner = 1
    while inner * inner * 4 <= count and count % (inner * 2) == 0:
        inner *= 2
    return inner, count // inner


def gather_kernel(z_hbm, dual_hbm, pix_ref, start_ref, z_v, dual_v, z_sem, dual_sem):
    slices, nblk, block = start_ref.shape
    col_blocks = z_hbm.shape[2] // block
    copies = []
    for n in range(nblk):
        pixel = pix_ref[0, n]
        row = pl.multiple_of(lax.div(pixel, col_blocks * 8) * 8, 8)
        col = pl.multiple_of(lax.rem(pixel, col_blocks) * block, block)
        at = (slice(None), pl.ds(row, 8), pl.ds(col, block))
        copies.append(pltpu.make_async_copy(z_hbm.at[at], z_v.at[n], z_sem.at[n]))
        copies.append(pltpu.make_async_copy(dual_hbm.at[(0, *at)], dual_v.at[n], dual_sem.at[n]))
    for copy in copies:
        copy.start()
    for copy in copies:
        copy.wait()
    sublanes = lax.broadcasted_iota(jnp.int32, (8, block), 0)
    tile_rows = lax.broadcasted_iota(jnp.int32, (nblk, block), 0)
    for s in range(slices):
        start = jnp.zeros((nblk, block), jnp.float32)
        for n in range(nblk):
            row = lax.rem(lax.div(pix_ref[0, n], col_blocks), 8)
            part = jnp.where(sublanes == row, z_v[n, s] - dual_v[n, s], 0.0)
            start = jnp.where(tile_rows == n, jnp.sum(part, axis=0, keepdims=True), start)
        start_ref[s] = start


def rays_kernel(
    sub_n, slab_n,
    z_hbm, start_ref, tile_hbm, meas_ref, ray_ref, pix_ref, step_ref,
    delta_out, pix_out, halo_out,
    tile_v, pix_v, got_in, got_out, delta_v, pixels_v, halo_v,
    load_sem, in_send, in_recv, out_send, out_recv,
    pix_send, pix_recv, halo_send, halo_recv, fin_send, fin_recv,
):
    slices, rows, width = z_hbm.shape
    nblk, block = tile_v.shape[0], tile_v.shape[1]
    ray_blocks = got_in.shape[2]
    col_blocks = width // block
    inner, outer = split_group(slab_n)
    sub = lax.axis_index("subset")
    slab = lax.axis_index("slab")
    lane = slab % inner
    tier = slab // inner
    has_up = slab > 0
    has_down = slab < slab_n - 1

    load = pltpu.make_async_copy(tile_hbm.at[0], tile_v, load_sem)
    load.start()

    pixels_v[...] = jnp.zeros_like(pixels_v)
    delta_v[...] = jnp.zeros_like(delta_v)
    halo_v[...] = jnp.zeros_like(halo_v)

    in_peers = [(sub, tier * inner + (lane + k) % inner) for k in range(1, inner)]
    out_peers = [(sub, ((tier + k) % outer) * inner + lane) for k in range(1, outer)]
    sub_peers = [((sub + k) % sub_n, slab) for k in range(1, sub_n)]
    barrier = pltpu.get_barrier_semaphore()
    for peer in in_peers + out_peers + sub_peers:
        pl.semaphore_signal(barrier, inc=1, device_id=peer, device_id_type=MESH)

    @pl.when(has_up)
    def _():
        for k in range(sub_n):
            pl.semaphore_signal(
                barrier, inc=1, device_id=((sub + k) % sub_n, slab - 1), device_id_type=MESH
            )

    @pl.when(has_down)
    def _():
        for k in range(sub_n):
            pl.semaphore_signal(
                barrier, inc=1, device_id=((sub + k) % sub_n, slab + 1), device_id_type=MESH
            )

    lanes = lax.broadcasted_iota(jnp.int32, (8, block), 1)
    mine = jnp.zeros((8, block), jnp.int32)
    for n in range(nblk):
        mine = jnp.where(lanes == n, pix_ref[0, n], mine)
    pix_v[...] = mine
    pixels_v[0, sub] = mine

    ray_rows = lax.broadcasted_iota(jnp.int32, (ray_blocks, block), 0)
    hot_rows = lax.broadcasted_iota(jnp.int32, (nblk, ray_blocks), 0)
    hot_cols = lax.broadcasted_iota(jnp.int32, (nblk, ray_blocks), 1)
    hot = jnp.zeros((nblk, ray_blocks), jnp.float32)
    for n in range(nblk):
        here = jnp.where(hot_cols == ray_ref[0, n], 1.0, 0.0)
        hot = jnp.where(hot_rows == n, here, hot)
    hot = hot.astype(jnp.bfloat16)
    load.wait()
    for s in range(slices):
        start = start_ref[s].astype(jnp.bfloat16)
        total = jnp.zeros((ray_blocks, block), jnp.float32)
        for n in range(nblk):
            term = lax.dot_general(
                start, tile_v[n], (((1,), (1,)), ((), ())), preferred_element_type=jnp.float32
            )
            total = total + jnp.where(ray_rows == ray_ref[0, n], term[n : n + 1], 0.0)
        got_in[lane, s] = total

    pl.semaphore_wait(
        barrier,
        len(in_peers + out_peers + sub_peers)
        + sub_n * (has_up.astype(jnp.int32) + has_down.astype(jnp.int32)),
    )

    def spread(src, dst, peers, send, recv):
        return [
            pltpu.make_async_remote_copy(
                src_ref=src, dst_ref=dst, send_sem=send.at[k], recv_sem=recv.at[k],
                device_id=peer, device_id_type=MESH,
            )
            for k, peer in enumerate(peers)
        ]

    ins = spread(got_in.at[lane], got_in.at[lane], in_peers, in_send, in_recv)
    for copy in ins:
        copy.start()

    pix_subs = spread(pix_v, pixels_v.at[0, sub], sub_peers, pix_send.at[0], pix_recv.at[0])
    above = [((sub + k) % sub_n, slab - 1) for k in range(sub_n)]
    below = [((sub + k) % sub_n, slab + 1) for k in range(sub_n)]
    pix_up = spread(pix_v, pixels_v.at[2, sub], above, pix_send.at[1], pix_recv.at[1])
    pix_down = spread(pix_v, pixels_v.at[1, sub], below, pix_send.at[2], pix_recv.at[2])
    halo_up = spread(
        z_hbm.at[:, pl.ds(0, 1)], halo_v.at[1], above[:1], halo_send.at[0], halo_recv.at[0]
    )
    halo_down = spread(
        z_hbm.at[:, pl.ds(rows - 1, 1)], halo_v.at[0], below[:1], halo_send.at[1], halo_recv.at[1]
    )
    for copy in pix_subs:
        copy.start()

    @pl.when(has_up)
    def _():
        for copy in pix_up + halo_up:
            copy.start()

    @pl.when(has_down)
    def _():
        for copy in pix_down + halo_down:
            copy.start()

    for copy in ins:
        copy.wait_recv()
    group = got_in[0]
    for k in range(1, inner):
        group = group + got_in[k]
    got_out[tier] = group
    outs = spread(got_out.at[tier], got_out.at[tier], out_peers, out_send, out_recv)
    for copy in outs:
        copy.start()
    targets = []
    for s in range(slices):
        target = jnp.zeros((ray_blocks, block), jnp.float32)
        for k in range(ray_blocks):
            piece = meas_ref[0, pl.ds(s, 1), pl.ds(k * block, block)]
            target = jnp.where(ray_rows == k, piece, target)
        targets.append(target)
    for copy in outs:
        copy.wait_recv()
    full = got_out[0]
    for k in range(1, outer):
        full = full + got_out[k]
    scale = step_ref[0] * (width / math.sqrt(ray_blocks * block))
    tile_rows = lax.broadcasted_iota(jnp.int32, (nblk, block), 0)
    for s in range(slices):
        residual = (full[s] - targets[s]).astype(jnp.bfloat16)
        picked = jnp.dot(hot, residual, preferred_element_type=jnp.float32).astype(jnp.bfloat16)
        delta = jnp.zeros((nblk, block), jnp.float32)
        for n in range(nblk):
            term = jnp.dot(picked, tile_v[n], preferred_element_type=jnp.float32)
            delta = jnp.where(tile_rows == n, term, delta)
        delta = delta * scale
        delta_v[0, sub, s] = delta

    own = delta_v.at[0, sub]
    fin_subs = spread(own, delta_v.at[0, sub], sub_peers, fin_send.at[0], fin_recv.at[0])
    fin_up = spread(own, delta_v.at[2, sub], above, fin_send.at[1], fin_recv.at[1])
    fin_down = spread(own, delta_v.at[1, sub], below, fin_send.at[2], fin_recv.at[2])

    @pl.when(has_up)
    def _():
        for copy in fin_up:
            copy.start()

    @pl.when(has_down)
    def _():
        for copy in fin_down:
            copy.start()

    for copy in fin_subs:
        copy.start()
    for copy in ins + outs:
        copy.wait_send()
    for copy in pix_subs + fin_subs:
        copy.wait()

    @pl.when(has_up)
    def _():
        for copy in pix_up + halo_up + fin_up:
            copy.wait_send()
        for copy in pix_down + halo_down + fin_down:
            copy.wait_recv()

    @pl.when(has_down)
    def _():
        for copy in pix_down + halo_down + fin_down:
            copy.wait_send()
        for copy in pix_up + halo_up + fin_up:
            copy.wait_recv()

    delta_out[...] = delta_v[...]
    pix_out[...] = pixels_v[...]
    halo_out[...] = halo_v[...]


def field_kernel(
    z_hbm, delta_ref, pix_ref, halo_ref, w_ref,
    field_hbm, dual_hbm,
    avg_v, own_v, field_v, dual_v, load_sem, store_sem,
):
    slices, rows, width = own_v.shape
    sub_n, nblk, block = delta_ref.shape[1], delta_ref.shape[3], delta_ref.shape[4]
    col_blocks = width // block
    sub = lax.axis_index("subset")
    loads = [
        pltpu.make_async_copy(z_hbm, avg_v.at[:, pl.ds(8, rows)], load_sem.at[0]),
        pltpu.make_async_copy(z_hbm, own_v, load_sem.at[1]),
    ]
    for load in loads:
        load.start()
    avg_v[:, pl.ds(7, 1), :] = halo_ref[0]
    avg_v[:, pl.ds(8 + rows, 1), :] = halo_ref[1]
    for load in loads:
        load.wait()
    share = 1.0 / sub_n
    sublanes = lax.broadcasted_iota(jnp.int32, (8, block), 0)
    for place in range(3):
        for i in range(sub_n):
            for n in range(nblk):
                pixel = pix_ref[place, i, 0, n]
                row = pixel // col_blocks
                col = pl.multiple_of((pixel % col_blocks) * block, block)
                if place == 0:
                    row = row + 8
                elif place == 1:
                    row = jnp.where(row == rows - 1, 7, 0)
                else:
                    row = jnp.where(row == 0, 8 + rows, 0)
                base = pl.multiple_of(row // 8 * 8, 8)
                for s in range(slices):
                    at = (s, pl.ds(base, 8), pl.ds(col, block))
                    value = delta_ref[place, i, s, pl.ds(n, 1), :] * share
                    avg_v[at] = avg_v[at] - jnp.where(sublanes == row % 8, value, 0.0)
    for n in range(nblk):
        pixel = pix_ref[0, sub, 0, n]
        row = pixel // col_blocks
        col = pl.multiple_of((pixel % col_blocks) * block, block)
        base = pl.multiple_of(row // 8 * 8, 8)
        for s in range(slices):
            at = (s, pl.ds(base, 8), pl.ds(col, block))
            value = delta_ref[0, sub, s, pl.ds(n, 1), :]
            own_v[at] = own_v[at] - jnp.where(sublanes == row % 8, value, 0.0)

    columns = lax.broadcasted_iota(jnp.int32, (8, width), 1)
    weights = [[[w_ref[a, b, c] for c in range(3)] for b in range(3)] for a in range(3)]

    def copies(s, g):
        at = pl.ds(pl.multiple_of(g * 8, 8), 8)
        return (
            pltpu.make_async_copy(field_v.at[s, at], field_hbm.at[s, at], store_sem.at[0]),
            pltpu.make_async_copy(dual_v.at[s, at], dual_hbm.at[0, s, at], store_sem.at[1]),
        )

    for s in range(slices):
        def step(g, carry, s=s):
            base = pl.multiple_of(g * 8, 8)
            at = pl.ds(base, 8)
            sums = [None, None, None]
            for a in range(3):
                if not 0 <= s + a - 1 < slices:
                    continue
                window = avg_v[s + a - 1, pl.ds(base, 24), :]
                for b in range(3):
                    moved = window[7 + b : 15 + b]
                    if a == 1 and b == 1:
                        middle = moved
                    for c in range(3):
                        term = weights[a][b][c] * moved
                        sums[c] = term if sums[c] is None else sums[c] + term
            left = jnp.where(columns == 0, 0.0, pltpu.roll(sums[0], 1, 1))
            right = jnp.where(columns == width - 1, 0.0, pltpu.roll(sums[2], width - 1, 1))
            field = middle + (sums[1] + left + right)
            field_v[s, at] = field
            dual_v[s, at] = own_v[s, at] - field
            for copy in copies(s, g):
                copy.start()
            return carry

        lax.fori_loop(0, rows // 8, step, 0)
    pltpu.make_async_copy(field_v, field_hbm, store_sem.at[0]).wait()
    pltpu.make_async_copy(dual_v, dual_hbm.at[0], store_sem.at[1]).wait()


def body(sub_n, slab_n, z_field, duals, tiles, ray_index, pixel_index, measured, step_size, kernel):
    slices, rows, width = z_field.shape
    nblk, block = tiles.shape[1], tiles.shape[2]
    ray_blocks = measured.shape[2] // block
    inner, outer = split_group(slab_n)
    hbm = pl.BlockSpec(memory_space=pl.ANY)
    vmem = pl.BlockSpec(memory_space=pltpu.VMEM)
    smem = pl.BlockSpec(memory_space=pltpu.SMEM)
    dma = pltpu.SemaphoreType.DMA
    delta_shape = (3, sub_n, slices, nblk, block)
    pix_shape = (3, sub_n, 8, block)
    halo_shape = (2, slices, 1, width)
    start = pl.pallas_call(
        gather_kernel,
        out_shape=jax.ShapeDtypeStruct((slices, nblk, block), jnp.float32),
        in_specs=[hbm, hbm, smem],
        out_specs=vmem,
        scratch_shapes=[
            pltpu.VMEM((nblk, slices, 8, block), jnp.float32),
            pltpu.VMEM((nblk, slices, 8, block), jnp.float32),
            dma((nblk,)), dma((nblk,)),
        ],
        name="gather",
    )(z_field, duals, pixel_index)
    delta, pixels, halo = pl.pallas_call(
        functools.partial(rays_kernel, sub_n, slab_n),
        out_shape=(
            jax.ShapeDtypeStruct(delta_shape, jnp.float32),
            jax.ShapeDtypeStruct(pix_shape, jnp.int32),
            jax.ShapeDtypeStruct(halo_shape, jnp.float32),
        ),
        in_specs=[hbm, vmem, hbm, vmem, smem, smem, smem],
        out_specs=(vmem, vmem, vmem),
        scratch_shapes=[
            pltpu.VMEM((nblk, block, block), jnp.bfloat16),
            pltpu.VMEM((8, block), jnp.int32),
            pltpu.VMEM((inner, slices, ray_blocks, block), jnp.float32),
            pltpu.VMEM((outer, slices, ray_blocks, block), jnp.float32),
            pltpu.VMEM(delta_shape, jnp.float32),
            pltpu.VMEM(pix_shape, jnp.int32),
            pltpu.VMEM(halo_shape, jnp.float32),
            dma,
            dma((inner,)), dma((inner,)),
            dma((outer,)), dma((outer,)),
            dma((3, sub_n)), dma((3, sub_n)),
            dma((2, 1)), dma((2, 1)),
            dma((3, sub_n)), dma((3, sub_n)),
        ],
        compiler_params=pltpu.CompilerParams(collective_id=0, has_side_effects=True),
        name="rays",
    )(z_field, start, tiles, measured, ray_index, pixel_index, step_size)
    return pl.pallas_call(
        field_kernel,
        out_shape=(
            jax.ShapeDtypeStruct((slices, rows, width), jnp.float32),
            jax.ShapeDtypeStruct((1, slices, rows, width), jnp.float32),
        ),
        in_specs=[hbm, vmem, smem, vmem, smem],
        out_specs=(hbm, hbm),
        scratch_shapes=[
            pltpu.VMEM((slices, rows + 16, width), jnp.float32),
            pltpu.VMEM((slices, rows, width), jnp.float32),
            pltpu.VMEM((slices, rows, width), jnp.float32),
            pltpu.VMEM((slices, rows, width), jnp.float32),
            dma((2,)), dma((2,)),
        ],
        name="field",
    )(z_field, delta, pixels, halo, kernel)


def solution(mesh):
    placed = (
        P(None, "slab", None),
        P("subset", None, "slab", None),
        P("subset", "slab", None, None),
        P("subset", "slab"),
        P("subset", "slab"),
        P("subset", None, None),
        P("subset"),
        P(),
    )
    return jax.shard_map(
        functools.partial(body, mesh.shape["subset"], mesh.shape["slab"]),
        mesh=mesh,
        in_specs=placed,
        out_specs=(P(None, "slab", None), P("subset", None, "slab", None)),
        check_vma=False,
    )
```

time: 243 us -> 27.2 us (0.11)
  matrix products: 77.4 us -> 0 us
  other arithmetic: 51.3 us -> 0 us
  blocking collectives: 44 us -> 0 us
  local copies, waits for them, and re-layouts: 30.3 us -> 0 us
  Pallas kernels: 0 us -> 25.6 us
  waiting for transfers between devices: 19.7 us -> 0 us
  between operations: 14.8 us -> 1.29 us
  starting transfers between devices: 4.99 us -> 0 us
    dot_general x5 -> x0, matrix products: 77.4 us -> none  [the longest x1 74.3 us: body(): jnp.einsum('abc,abcsrw->srw', kernel, full_stack, precision=lax.Precision...]
    psum x1 -> x0, blocking collectives: 44 us -> none  [body(): total_rays = lax.psum(partial_rays, 'slab')]
    another operation x4 -> x0, other arithmetic: 40.2 us -> none  [the longest x1 20.5 us: body(): jnp.stack([column_stack[:, :, offset_b:offset_b + row_count] for offset_b...]
    another operation x3 -> x0, local copies, waits for them, and re-layouts: 27.3 us -> none  [the longest x1 14.3 us: body(): jnp.stack([row_stack[:, :, offset_a:offset_a + slice_count] for offset_a...]
    pallas_call x0 -> x3, Pallas kernels: none -> 25.6 us  [the longest x1 16.7 us: body(): pl.pallas_call(functools.partial(rays_kernel, sub_n, slab_n), out_shape=(...]
    psum x1 -> x0, waiting for transfers between devices: 15.4 us -> none  [body(): average = lax.psum(estimate + dual_part, 'subset') / lax.axis_size('subset')]
    ppermute x2 -> x0, starting transfers between devices: 4.95 us -> none  [the longest x1 3.66 us: extended(): before = lax.ppermute(last, axis, up)]
    ppermute x2 -> x0, waiting for transfers between devices: 4.24 us -> none  [the longest x1 4.2 us: extended(): after = lax.ppermute(first, axis, down)]
  transfers between devices with their start and end apart: 3 -> 0, of which waited for: 2 -> 0; matrix products, arithmetic and copies ran while one was open for 0% -> 0% of each run, Pallas kernels for 0% -> 0%
where the time goes in v1:
time: 27.2 us; the launch traced here: 26.8 us
  Pallas kernels  25.6 us (94%)
  between operations  1.29 us (5%)
    pallas_call x1, Pallas kernels, body(): pl.pallas_call(functools.partial(rays_kernel, sub_n, slab_n), out_shape=(...  16.7 us
    pallas_call x1, Pallas kernels, body(): pl.pallas_call(field_kernel, out_shape=(jax.ShapeDtypeStruct((slices, row...  6.55 us
    pallas_call x1, Pallas kernels, body(): pl.pallas_call(gather_kernel, out_shape=jax.ShapeDtypeStruct((slices, nbl...  2.3 us

profile of v1, /device:TPU:0, one launch (start us, length us, event | category | flops | bytes accessed | tf_op | source)
XLA Modules:
  0.0 26.8 jit_solution(6123526945520030919)
XLA Ops:
  1.3 2.3 %gather.1.start_ref = f32[1,8,128]{2,1,0:T(8,128)} custom-call(f32[1,128,2048]{2,1,0:T(8,128)} %z_hbm.5, f32[1,1,128,2048]{3,2,1,0:T(8,128)} %dual_hbm.1, s32[1,8]{1,0:T(1,128)} %pix_ref.3), custom_call_target="tpu_custom_call" | custom-call | tf_op jit(solution)/shard_map/gather/pallas_call | solution.py:338
  3.6 16.7 %rays.1 = (f32[3,2,1,8,128]{4,3,2,1,0:T(8,128)}, s32[3,2,8,128]{3,2,1,0:T(8,128)}, f32[2,1,1,2048]{3,2,1,0:T(1,128)}) custom-call(f32[1,128,2048]{2,1,0:T(8,128)} %z_hbm.5, f32[1,8,128]{2,1,0:T(8,128)} %gather.1.start_ref, bf16[1,8,128,128]{3,2,1,0:T(8,128)(2,1)} %tile_hbm.1, f32[1,1,2048]{2,1,0:T(1,128)} %meas_ref.1, s32[1,8]{1,0:T(1,128)} %ray_ref.1, ...), custom_call_target="tpu_custom_call" | custom-call | tf_op jit(solution)/shard_map/rays/pallas_call | solution.py:350
  20.3 6.5 %field.1 = (f32[1,128,2048]{2,1,0:T(8,128)}, f32[1,1,128,2048]{3,2,1,0:T(8,128)}) custom-call(f32[1,128,2048]{2,1,0:T(8,128)} %z_hbm.5, f32[3,2,1,8,128]{4,3,2,1,0:T(8,128)} %get-tuple-element.5.delta_ref, s32[3,2,8,128]{3,2,1,0:T(8,128)} %get-tuple-element.6.pix_ref, f32[2,1,1,2048]{3,2,1,0:T(1,128)} %get-tuple-element.7.halo_ref, f32[3,3,3]{2,1,0:T(4,128)} %w_ref.1), custom_call_target="tpu_custom_call" | custom-call | tf_op jit(solution)/shard_map/field/pallas_call | solution.py:377

commit v2 on v1

v2 whole, which is shorter than its diff:
```python
import functools
import math

import jax
import jax.numpy as jnp
from jax import lax
from jax.experimental import pallas as pl
from jax.experimental.pallas import tpu as pltpu
from jax.sharding import PartitionSpec as P

MESH = pl.DeviceIdType.MESH


def split_group(count):
    inner = 1
    while inner < min(count, 16) and count % (inner * 2) == 0:
        inner *= 2
    return inner, count // inner


def rays_kernel(
    sub_n, slab_n,
    z_hbm, dual_hbm, tile_hbm, meas_hbm, ray_hbm, pix_hbm, step_hbm, w_hbm,
    delta_out, pix_out, base_out,
    meas_ref, ray_ref, pix_ref, step_ref, w_ref, z_v, dual_v, base_v, tile_v, pix_v, got_in, got_out, delta_v, pixels_v, halo_v,
    load_sem, base_sem, in_send, in_recv, out_send, out_recv,
    pix_send, pix_recv, halo_send, halo_recv, fin_send, fin_recv,
):
    slices, rows, width = z_hbm.shape
    nblk, block = tile_v.shape[0], tile_v.shape[1]
    ray_blocks = got_in.shape[2]
    col_blocks = width // block
    inner, outer = split_group(slab_n)
    sub = lax.axis_index("subset")
    slab = lax.axis_index("slab")
    lane = slab % inner
    tier = slab // inner
    has_up = slab > 0
    has_down = slab < slab_n - 1

    loads = [
        pltpu.make_async_copy(z_hbm, z_v.at[:, pl.ds(8, rows)], load_sem.at[0]),
        pltpu.make_async_copy(dual_hbm.at[0], dual_v, load_sem.at[1]),
        pltpu.make_async_copy(tile_hbm.at[0], tile_v, load_sem.at[2]),
    ]
    pairs = [
        (meas_hbm, meas_ref), (ray_hbm, ray_ref), (pix_hbm, pix_ref),
        (step_hbm, step_ref), (w_hbm, w_ref),
    ]
    smalls = [
        pltpu.make_async_copy(src, dst, load_sem.at[3 + i]) for i, (src, dst) in enumerate(pairs)
    ]
    for load in smalls + loads:
        load.start()

    pixels_v[...] = jnp.zeros_like(pixels_v)
    delta_v[...] = jnp.zeros_like(delta_v)
    halo_v[...] = jnp.zeros_like(halo_v)

    in_peers = [(sub, tier * inner + (lane + k) % inner) for k in range(1, inner)]
    out_peers = [(sub, ((tier + k) % outer) * inner + lane) for k in range(1, outer)]
    sub_peers = [((sub + k) % sub_n, slab) for k in range(1, sub_n)]
    barrier = pltpu.get_barrier_semaphore()
    for peer in in_peers + out_peers + sub_peers:
        pl.semaphore_signal(barrier, inc=1, device_id=peer, device_id_type=MESH)

    @pl.when(has_up)
    def _():
        for k in range(sub_n):
            pl.semaphore_signal(
                barrier, inc=1, device_id=((sub + k) % sub_n, slab - 1), device_id_type=MESH
            )

    @pl.when(has_down)
    def _():
        for k in range(sub_n):
            pl.semaphore_signal(
                barrier, inc=1, device_id=((sub + k) % sub_n, slab + 1), device_id_type=MESH
            )

    for load in smalls:
        load.wait()
    columns = lax.broadcasted_iota(jnp.int32, (8, width), 1)
    weights = [[[w_ref[a, b, c] for c in range(3)] for b in range(3)] for a in range(3)]

    def stencil(low, high):
        for s in range(slices):
            def step(g, carry, s=s):
                base = pl.multiple_of(g * 8, 8)
                sums = [None, None, None]
                for a in range(3):
                    if not 0 <= s + a - 1 < slices:
                        continue
                    window = z_v[s + a - 1, pl.ds(base, 24), :]
                    for b in range(3):
                        moved = window[7 + b : 15 + b]
                        if a == 1 and b == 1:
                            middle = moved
                        for c in range(3):
                            term = weights[a][b][c] * moved
                            sums[c] = term if sums[c] is None else sums[c] + term
                left = jnp.where(columns == 0, 0.0, pltpu.roll(sums[0], 1, 1))
                right = jnp.where(columns == width - 1, 0.0, pltpu.roll(sums[2], width - 1, 1))
                base_v[s, pl.ds(base, 8), :] = middle + (sums[1] + left + right)
                return carry

            lax.fori_loop(low, high, step, 0)

    groups = rows // 8
    first_cut = 1 + max(groups - 2, 0) * 5 // 14
    second_cut = 1 + max(groups - 2, 0) * 10 // 14

    lanes = lax.broadcasted_iota(jnp.int32, (8, block), 1)
    mine = jnp.zeros((8, block), jnp.int32)
    for n in range(nblk):
        mine = jnp.where(lanes == n, pix_ref[0, n], mine)
    pix_v[...] = mine
    pixels_v[0, sub] = mine

    ray_rows = lax.broadcasted_iota(jnp.int32, (ray_blocks, block), 0)
    hot_rows = lax.broadcasted_iota(jnp.int32, (nblk, ray_blocks), 0)
    hot_cols = lax.broadcasted_iota(jnp.int32, (nblk, ray_blocks), 1)
    hot = jnp.zeros((nblk, ray_blocks), jnp.float32)
    for n in range(nblk):
        here = jnp.where(hot_cols == ray_ref[0, n], 1.0, 0.0)
        hot = jnp.where(hot_rows == n, here, hot)
    hot = hot.astype(jnp.bfloat16)
    row_cols = lax.broadcasted_iota(jnp.int32, (nblk, rows), 1)
    row_rows = lax.broadcasted_iota(jnp.int32, (nblk, rows), 0)
    tile_rows = lax.broadcasted_iota(jnp.int32, (nblk, block), 0)
    row_hot = jnp.zeros((nblk, rows), jnp.float32)
    col_of = jnp.zeros((nblk, block), jnp.int32)
    for n in range(nblk):
        here = jnp.where(row_cols == lax.div(pix_ref[0, n], col_blocks), 1.0, 0.0)
        row_hot = jnp.where(row_rows == n, here, row_hot)
        col_of = jnp.where(tile_rows == n, lax.rem(pix_ref[0, n], col_blocks), col_of)
    row_hot = row_hot.astype(jnp.bfloat16)
    for load in loads:
        load.wait()
    for s in range(slices):
        start = jnp.zeros((nblk, block), jnp.float32)
        for c in range(col_blocks):
            at = pl.ds(c * block, block)
            part = (z_v[s, pl.ds(8, rows), at] - dual_v[s, :, at]).astype(jnp.bfloat16)
            part = jnp.dot(row_hot, part, preferred_element_type=jnp.float32)
            start = jnp.where(col_of == c, part, start)
        start = start.astype(jnp.bfloat16)
        total = jnp.zeros((ray_blocks, block), jnp.float32)
        for n in range(nblk):
            term = lax.dot_general(
                start, tile_v[n], (((1,), (1,)), ((), ())), preferred_element_type=jnp.float32
            )
            total = total + jnp.where(ray_rows == ray_ref[0, n], term[n : n + 1], 0.0)
        got_in[lane, s] = total

    pl.semaphore_wait(
        barrier,
        len(in_peers + out_peers + sub_peers)
        + sub_n * (has_up.astype(jnp.int32) + has_down.astype(jnp.int32)),
    )

    def spread(src, dst, peers, send, recv):
        return [
            pltpu.make_async_remote_copy(
                src_ref=src, dst_ref=dst, send_sem=send.at[k], recv_sem=recv.at[k],
                device_id=peer, device_id_type=MESH,
            )
            for k, peer in enumerate(peers)
        ]

    ins = spread(got_in.at[lane], got_in.at[lane], in_peers, in_send, in_recv)
    for copy in ins:
        copy.start()

    pix_subs = spread(pix_v, pixels_v.at[0, sub], sub_peers, pix_send.at[0], pix_recv.at[0])
    above = [((sub + k) % sub_n, slab - 1) for k in range(sub_n)]
    below = [((sub + k) % sub_n, slab + 1) for k in range(sub_n)]
    pix_up = spread(pix_v, pixels_v.at[2, sub], above, pix_send.at[1], pix_recv.at[1])
    pix_down = spread(pix_v, pixels_v.at[1, sub], below, pix_send.at[2], pix_recv.at[2])
    halo_up = spread(
        z_hbm.at[:, pl.ds(0, 1)], halo_v.at[1], above[:1], halo_send.at[0], halo_recv.at[0]
    )
    halo_down = spread(
        z_hbm.at[:, pl.ds(rows - 1, 1)], halo_v.at[0], below[:1], halo_send.at[1], halo_recv.at[1]
    )
    for copy in pix_subs:
        copy.start()

    @pl.when(has_up)
    def _():
        for copy in pix_up + halo_up:
            copy.start()

    @pl.when(has_down)
    def _():
        for copy in pix_down + halo_down:
            copy.start()

    stencil(1, first_cut)
    for copy in ins:
        copy.wait_recv()
    group = got_in[0]
    for k in range(1, inner):
        group = group + got_in[k]
    got_out[tier] = group
    outs = spread(got_out.at[tier], got_out.at[tier], out_peers, out_send, out_recv)
    for copy in outs:
        copy.start()
    targets = []
    for s in range(slices):
        target = jnp.zeros((ray_blocks, block), jnp.float32)
        for k in range(ray_blocks):
            piece = meas_ref[0, pl.ds(s, 1), pl.ds(k * block, block)]
            target = jnp.where(ray_rows == k, piece, target)
        targets.append(target)
    stencil(first_cut, second_cut)
    for copy in outs:
        copy.wait_recv()
    full = got_out[0]
    for k in range(1, outer):
        full = full + got_out[k]
    scale = step_ref[0] * (width / math.sqrt(ray_blocks * block))
    for s in range(slices):
        residual = (full[s] - targets[s]).astype(jnp.bfloat16)
        picked = jnp.dot(hot, residual, preferred_element_type=jnp.float32).astype(jnp.bfloat16)
        delta = jnp.zeros((nblk, block), jnp.float32)
        for n in range(nblk):
            term = jnp.dot(picked, tile_v[n], preferred_element_type=jnp.float32)
            delta = jnp.where(tile_rows == n, term, delta)
        delta = delta * scale
        delta_v[0, sub, s] = delta

    own = delta_v.at[0, sub]
    fin_subs = spread(own, delta_v.at[0, sub], sub_peers, fin_send.at[0], fin_recv.at[0])
    fin_up = spread(own, delta_v.at[2, sub], above, fin_send.at[1], fin_recv.at[1])
    fin_down = spread(own, delta_v.at[1, sub], below, fin_send.at[2], fin_recv.at[2])

    @pl.when(has_up)
    def _():
        for copy in fin_up:
            copy.start()

    @pl.when(has_down)
    def _():
        for copy in fin_down:
            copy.start()

    for copy in fin_subs:
        copy.start()
    stencil(second_cut, max(groups - 1, 1))

    @pl.when(has_down)
    def _():
        for copy in halo_up:
            copy.wait_recv()

    @pl.when(has_up)
    def _():
        for copy in halo_down:
            copy.wait_recv()

    z_v[:, pl.ds(7, 1), :] = halo_v[0]
    z_v[:, pl.ds(8 + rows, 1), :] = halo_v[1]
    stencil(0, 1)
    if groups > 1:
        stencil(groups - 1, groups)
    base_copy = pltpu.make_async_copy(base_v, base_out, base_sem)
    base_copy.start()
    for copy in ins + outs:
        copy.wait_send()
    for copy in pix_subs + fin_subs:
        copy.wait()

    @pl.when(has_up)
    def _():
        for copy in pix_up + halo_up + fin_up:
            copy.wait_send()
        for copy in pix_down + fin_down:
            copy.wait_recv()

    @pl.when(has_down)
    def _():
        for copy in pix_down + halo_down + fin_down:
            copy.wait_send()
        for copy in pix_up + fin_up:
            copy.wait_recv()

    delta_out[...] = delta_v[...]
    pix_out[...] = pixels_v[...]
    base_copy.wait()


def field_kernel(
    z_hbm, base_hbm, delta_ref, pix_ref, w_ref,
    field_hbm, dual_hbm,
    field_v, own_v, load_sem, store_sem,
):
    slices, rows, width = own_v.shape
    sub_n, nblk, block = delta_ref.shape[1], delta_ref.shape[3], delta_ref.shape[4]
    col_blocks = width // block
    sub = lax.axis_index("subset")
    inside = (slice(None), pl.ds(8, rows), pl.ds(block, width))
    loads = [
        pltpu.make_async_copy(base_hbm, field_v.at[inside], load_sem.at[0]),
        pltpu.make_async_copy(z_hbm, own_v, load_sem.at[1]),
    ]
    for load in loads:
        load.start()
    weights = [[[w_ref[a, b, c] for c in range(3)] for b in range(3)] for a in range(3)]
    share = -1.0 / sub_n
    sublanes = lax.broadcasted_iota(jnp.int32, (8, block), 0)
    window_rows = lax.broadcasted_iota(jnp.int32, (16, 3 * block), 0)
    zeros = jnp.zeros((1, block), jnp.float32)

    def patch(place, i, n, row, col):
        base = pl.multiple_of((row - 1) // 8 * 8, 8)
        step = window_rows - (row - 1 - base)
        for s in range(slices):
            delta = delta_ref[place, i, s, pl.ds(n, 1), :] * share
            wide = jnp.concatenate([zeros, delta, zeros], axis=1)
            left = pltpu.roll(wide, 1, 1)
            right = pltpu.roll(wide, 3 * block - 1, 1)
            for a in range(3):
                out = s + 1 - a
                if not 0 <= out < slices:
                    continue
                sums = [w[0] * left + w[1] * wide + w[2] * right for w in weights[a]]
                if a == 1:
                    sums[1] = sums[1] + wide
                add = jnp.where(step == 2, sums[0], 0.0)
                add = jnp.where(step == 1, sums[1], add)
                add = jnp.where(step == 0, sums[2], add)
                at = (out, pl.ds(base, 16), pl.ds(col, 3 * block))
                field_v[at] = field_v[at] + add

    for load in loads:
        load.wait()
    for place in range(3):
        for i in range(sub_n):
            for n in range(nblk):
                pixel = pix_ref[place, i, 0, n]
                row = pixel // col_blocks
                col = pl.multiple_of((pixel % col_blocks) * block, block)
                if place == 0:
                    patch(place, i, n, row + 8, col)
                elif place == 1:
                    pl.when(row == rows - 1)(functools.partial(patch, place, i, n, 7, col))
                else:
                    pl.when(row == 0)(functools.partial(patch, place, i, n, rows + 8, col))
    stores = [pltpu.make_async_copy(field_v.at[inside], field_hbm, store_sem.at[0])]
    stores[0].start()
    for n in range(nblk):
        pixel = pix_ref[0, sub, 0, n]
        row = pixel // col_blocks
        col = pl.multiple_of((pixel % col_blocks) * block, block)
        base = pl.multiple_of(row // 8 * 8, 8)
        for s in range(slices):
            at = (s, pl.ds(base, 8), pl.ds(col, block))
            value = delta_ref[0, sub, s, pl.ds(n, 1), :]
            own_v[at] = own_v[at] - jnp.where(sublanes == row % 8, value, 0.0)
    parts = 4 if rows % 32 == 0 else 1
    size = rows // parts
    for part in range(parts):
        for s in range(slices):
            def step(g, carry, s=s, part=part):
                at = pl.multiple_of(part * size + g * 8, 8)
                field = field_v[s, pl.ds(at + 8, 8), pl.ds(block, width)]
                own_v[s, pl.ds(at, 8), :] = own_v[s, pl.ds(at, 8), :] - field
                return carry

            lax.fori_loop(0, size // 8, step, 0)
        span = (slice(None), pl.ds(part * size, size))
        stores.append(
            pltpu.make_async_copy(own_v.at[span], dual_hbm.at[(0, *span)], store_sem.at[1 + part])
        )
        stores[-1].start()
    for store in stores:
        store.wait()


def body(sub_n, slab_n, z_field, duals, tiles, ray_index, pixel_index, measured, step_size, kernel):
    slices, rows, width = z_field.shape
    nblk, block = tiles.shape[1], tiles.shape[2]
    ray_blocks = measured.shape[2] // block
    inner, outer = split_group(slab_n)
    hbm = pl.BlockSpec(memory_space=pl.ANY)
    vmem = pl.BlockSpec(memory_space=pltpu.VMEM)
    smem = pl.BlockSpec(memory_space=pltpu.SMEM)
    dma = pltpu.SemaphoreType.DMA
    delta_shape = (3, sub_n, slices, nblk, block)
    pix_shape = (3, sub_n, 8, block)
    halo_shape = (2, slices, 1, width)
    delta, pixels, base = pl.pallas_call(
        functools.partial(rays_kernel, sub_n, slab_n),
        out_shape=(
            jax.ShapeDtypeStruct(delta_shape, jnp.float32),
            jax.ShapeDtypeStruct(pix_shape, jnp.int32),
            jax.ShapeDtypeStruct((slices, rows, width), jnp.float32),
        ),
        in_specs=[pl.BlockSpec(memory_space=pltpu.HBM)] * 8,
        out_specs=(vmem, vmem, hbm),
        scratch_shapes=[
            pltpu.VMEM(measured.shape, jnp.float32),
            pltpu.SMEM(ray_index.shape, jnp.int32),
            pltpu.SMEM(pixel_index.shape, jnp.int32),
            pltpu.SMEM(step_size.shape, jnp.float32),
            pltpu.SMEM(kernel.shape, jnp.float32),
            pltpu.VMEM((slices, rows + 16, width), jnp.float32),
            pltpu.VMEM((slices, rows, width), jnp.float32),
            pltpu.VMEM((slices, rows, width), jnp.float32),
            pltpu.VMEM((nblk, block, block), jnp.bfloat16),
            pltpu.VMEM((8, block), jnp.int32),
            pltpu.VMEM((inner, slices, ray_blocks, block), jnp.float32),
            pltpu.VMEM((outer, slices, ray_blocks, block), jnp.float32),
            pltpu.VMEM(delta_shape, jnp.float32),
            pltpu.VMEM(pix_shape, jnp.int32),
            pltpu.VMEM(halo_shape, jnp.float32),
            dma((8,)), dma,
            dma((inner,)), dma((inner,)),
            dma((outer,)), dma((outer,)),
            dma((3, sub_n)), dma((3, sub_n)),
            dma((2, 1)), dma((2, 1)),
            dma((3, sub_n)), dma((3, sub_n)),
        ],
        compiler_params=pltpu.CompilerParams(collective_id=0, has_side_effects=True),
        name="rays",
    )(z_field, duals, tiles, measured, ray_index, pixel_index, step_size, kernel)
    return pl.pallas_call(
        field_kernel,
        out_shape=(
            jax.ShapeDtypeStruct((slices, rows, width), jnp.float32),
            jax.ShapeDtypeStruct((1, slices, rows, width), jnp.float32),
        ),
        in_specs=[hbm, hbm, vmem, smem, smem],
        out_specs=(hbm, hbm),
        scratch_shapes=[
            pltpu.VMEM((slices, rows + 16, width + 2 * block), jnp.float32),
            pltpu.VMEM((slices, rows, width), jnp.float32),
            dma((2,)), dma((5,)),
        ],

        name="field",
    )(z_field, base, delta, pixels, kernel)


def solution(mesh):
    placed = (
        P(None, "slab", None),
        P("subset", None, "slab", None),
        P("subset", "slab", None, None),
        P("subset", "slab"),
        P("subset", "slab"),
        P("subset", None, None),
        P("subset"),
        P(),
    )
    return jax.shard_map(
        functools.partial(body, mesh.shape["subset"], mesh.shape["slab"]),
        mesh=mesh,
        in_specs=placed,
        out_specs=(P(None, "slab", None), P("subset", None, "slab", None)),
        check_vma=False,
    )
```

time: 27.2 us -> 22.2 us (0.82)
  Pallas kernels: 25.6 us -> 20.7 us
    pallas_call x1 -> x0, Pallas kernels: 2.3 us -> none  [body(): pl.pallas_call(gather_kernel, out_shape=jax.ShapeDtypeStruct((slices, nbl...]
    pallas_call x1, Pallas kernels: 6.55 us -> 4.98 us  [body(): pl.pallas_call(field_kernel, out_shape=(jax.ShapeDtypeStruct((slices, row...]
    pallas_call x1, Pallas kernels: 16.7 us -> 15.7 us  [body(): pl.pallas_call(functools.partial(rays_kernel, sub_n, slab_n), out_shape=(...]
where the time goes in v2:
time: 22.2 us; the launch traced here: 21.9 us
  Pallas kernels  20.7 us (93%)
  between operations  1.29 us (6%)
    pallas_call x1, Pallas kernels, body(): pl.pallas_call(functools.partial(rays_kernel, sub_n, slab_n), out_shape=(...  15.7 us
    pallas_call x1, Pallas kernels, body(): pl.pallas_call(field_kernel, out_shape=(jax.ShapeDtypeStruct((slices, row...  4.98 us

profile of v2, /device:TPU:0, one launch (start us, length us, event | category | flops | bytes accessed | tf_op | source)
XLA Modules:
  0.0 21.9 jit_solution(12043851117489764543)
XLA Ops:
  1.3 15.7 %rays.1 = (f32[3,2,1,8,128]{4,3,2,1,0:T(8,128)}, s32[3,2,8,128]{3,2,1,0:T(8,128)}, f32[1,128,2048]{2,1,0:T(8,128)}) custom-call(f32[1,128,2048]{2,1,0:T(8,128)} %z_hbm.3, f32[1,1,128,2048]{3,2,1,0:T(8,128)} %dual_hbm.1, bf16[1,8,128,128]{3,2,1,0:T(8,128)(2,1)} %tile_hbm.1, f32[1,1,2048]{2,1,0:T(1,128)} %meas_hbm.1, s32[1,8]{1,0:T(1,128)} %ray_hbm.1, ...), custom_call_target="tpu_custom_call" | custom-call | tf_op jit(solution)/shard_map/rays/pallas_call | solution.py:393
  17.0 5.0 %field.1 = (f32[1,128,2048]{2,1,0:T(8,128)}, f32[1,1,128,2048]{3,2,1,0:T(8,128)}) custom-call(f32[1,128,2048]{2,1,0:T(8,128)} %z_hbm.3, f32[1,128,2048]{2,1,0:T(8,128)} %get-tuple-element.5.base_hbm, f32[3,2,1,8,128]{4,3,2,1,0:T(8,128)} %get-tuple-element.6.delta_ref, s32[3,2,8,128]{3,2,1,0:T(8,128)} %get-tuple-element.7.pix_ref, f32[3,3,3]{2,1,0:T(4,128)} %w_ref.1), custom_call_target="tpu_custom_call" | custom-call | tf_op jit(solution)/shard_map/field/pallas_call | solution.py:428

commit v3 on v2

--- a/solution.py
+++ b/solution.py
@@ -8,6 +8,7 @@
 from jax.experimental.pallas import tpu as pltpu
 from jax.sharding import PartitionSpec as P
 
+
 MESH = pl.DeviceIdType.MESH
 
 
@@ -22,7 +23,7 @@
     sub_n, slab_n,
     z_hbm, dual_hbm, tile_hbm, meas_hbm, ray_hbm, pix_hbm, step_hbm, w_hbm,
     delta_out, pix_out, base_out,
-    meas_ref, ray_ref, pix_ref, step_ref, w_ref, z_v, dual_v, base_v, tile_v, pix_v, got_in, got_out, delta_v, pixels_v, halo_v,
+    meas_ref, ray_ref, pix_ref, step_ref, w_ref, z_v, dual_v, base_v, tile_v, pix_v, got_in, got_out, delta_v, halo_v,
     load_sem, base_sem, in_send, in_recv, out_send, out_recv,
     pix_send, pix_recv, halo_send, halo_recv, fin_send, fin_recv,
 ):
@@ -53,8 +54,6 @@
     for load in smalls + loads:
         load.start()
 
-    pixels_v[...] = jnp.zeros_like(pixels_v)
-    delta_v[...] = jnp.zeros_like(delta_v)
     halo_v[...] = jnp.zeros_like(halo_v)
 
     in_peers = [(sub, tier * inner + (lane + k) % inner) for k in range(1, inner)]
@@ -107,15 +106,14 @@
             lax.fori_loop(low, high, step, 0)
 
     groups = rows // 8
-    first_cut = 1 + max(groups - 2, 0) * 5 // 14
     second_cut = 1 + max(groups - 2, 0) * 10 // 14
+    first_cut = second_cut if outer == 1 else (1 + second_cut) // 2
 
     lanes = lax.broadcasted_iota(jnp.int32, (8, block), 1)
     mine = jnp.zeros((8, block), jnp.int32)
     for n in range(nblk):
         mine = jnp.where(lanes == n, pix_ref[0, n], mine)
     pix_v[...] = mine
-    pixels_v[0, sub] = mine
 
     ray_rows = lax.broadcasted_iota(jnp.int32, (ray_blocks, block), 0)
     hot_rows = lax.broadcasted_iota(jnp.int32, (nblk, ray_blocks), 0)
@@ -153,6 +151,14 @@
             total = total + jnp.where(ray_rows == ray_ref[0, n], term[n : n + 1], 0.0)
         got_in[lane, s] = total
 
+    targets = []
+    for s in range(slices):
+        target = jnp.zeros((ray_blocks, block), jnp.float32)
+        for k in range(ray_blocks):
+            piece = meas_ref[0, pl.ds(s, 1), pl.ds(k * block, block)]
+            target = jnp.where(ray_rows == k, piece, target)
+        targets.append(target)
+
     pl.semaphore_wait(
         barrier,
         len(in_peers + out_peers + sub_peers)
@@ -172,18 +178,19 @@
     for copy in ins:
         copy.start()
 
-    pix_subs = spread(pix_v, pixels_v.at[0, sub], sub_peers, pix_send.at[0], pix_recv.at[0])
+    pix_subs = spread(pix_v, pix_out.at[0, sub], sub_peers, pix_send.at[0], pix_recv.at[0])
     above = [((sub + k) % sub_n, slab - 1) for k in range(sub_n)]
     below = [((sub + k) % sub_n, slab + 1) for k in range(sub_n)]
-    pix_up = spread(pix_v, pixels_v.at[2, sub], above, pix_send.at[1], pix_recv.at[1])
-    pix_down = spread(pix_v, pixels_v.at[1, sub], below, pix_send.at[2], pix_recv.at[2])
+    pix_up = spread(pix_v, pix_out.at[2, sub], above, pix_send.at[1], pix_recv.at[1])
+    pix_down = spread(pix_v, pix_out.at[1, sub], below, pix_send.at[2], pix_recv.at[2])
     halo_up = spread(
         z_hbm.at[:, pl.ds(0, 1)], halo_v.at[1], above[:1], halo_send.at[0], halo_recv.at[0]
     )
     halo_down = spread(
         z_hbm.at[:, pl.ds(rows - 1, 1)], halo_v.at[0], below[:1], halo_send.at[1], halo_recv.at[1]
     )
-    for copy in pix_subs:
+    keeps = [pltpu.make_async_copy(pix_v, pix_out.at[0, sub], base_sem.at[0])]
+    for copy in keeps + pix_subs:
         copy.start()
 
     @pl.when(has_up)
@@ -206,13 +213,6 @@
     outs = spread(got_out.at[tier], got_out.at[tier], out_peers, out_send, out_recv)
     for copy in outs:
         copy.start()
-    targets = []
-    for s in range(slices):
-        target = jnp.zeros((ray_blocks, block), jnp.float32)
-        for k in range(ray_blocks):
-            piece = meas_ref[0, pl.ds(s, 1), pl.ds(k * block, block)]
-            target = jnp.where(ray_rows == k, piece, target)
-        targets.append(target)
     stencil(first_cut, second_cut)
     for copy in outs:
         copy.wait_recv()
@@ -228,12 +228,11 @@
             term = jnp.dot(picked, tile_v[n], preferred_element_type=jnp.float32)
             delta = jnp.where(tile_rows == n, term, delta)
         delta = delta * scale
-        delta_v[0, sub, s] = delta
-
-    own = delta_v.at[0, sub]
-    fin_subs = spread(own, delta_v.at[0, sub], sub_peers, fin_send.at[0], fin_recv.at[0])
-    fin_up = spread(own, delta_v.at[2, sub], above, fin_send.at[1], fin_recv.at[1])
-    fin_down = spread(own, delta_v.at[1, sub], below, fin_send.at[2], fin_recv.at[2])
+        delta_v[s] = delta
+
+    fin_subs = spread(delta_v, delta_out.at[0, sub], sub_peers, fin_send.at[0], fin_recv.at[0])
+    fin_up = spread(delta_v, delta_out.at[2, sub], above, fin_send.at[1], fin_recv.at[1])
+    fin_down = spread(delta_v, delta_out.at[1, sub], below, fin_send.at[2], fin_recv.at[2])
 
     @pl.when(has_up)
     def _():
@@ -245,7 +244,8 @@
         for copy in fin_down:
             copy.start()
 
-    for copy in fin_subs:
+    keeps.append(pltpu.make_async_copy(delta_v, delta_out.at[0, sub], base_sem.at[1]))
+    for copy in fin_subs + keeps[1:]:
         copy.start()
     stencil(second_cut, max(groups - 1, 1))
 
@@ -264,8 +264,8 @@
     stencil(0, 1)
     if groups > 1:
         stencil(groups - 1, groups)
-    base_copy = pltpu.make_async_copy(base_v, base_out, base_sem)
-    base_copy.start()
+    keeps.append(pltpu.make_async_copy(base_v, base_out, base_sem.at[2]))
+    keeps[2].start()
     for copy in ins + outs:
         copy.wait_send()
     for copy in pix_subs + fin_subs:
@@ -285,27 +285,34 @@
         for copy in pix_up + fin_up:
             copy.wait_recv()
 
-    delta_out[...] = delta_v[...]
-    pix_out[...] = pixels_v[...]
-    base_copy.wait()
+    for copy in keeps:
+        copy.wait()
 
 
 def field_kernel(
-    z_hbm, base_hbm, delta_ref, pix_ref, w_ref,
+    slab_n, z_hbm, base_hbm, delta_hbm, pix_hbm, w_hbm,
     field_hbm, dual_hbm,
-    field_v, own_v, load_sem, store_sem,
+    delta_ref, pix_ref, w_ref, field_v, own_v, load_sem, store_sem,
 ):
     slices, rows, width = own_v.shape
     sub_n, nblk, block = delta_ref.shape[1], delta_ref.shape[3], delta_ref.shape[4]
     col_blocks = width // block
     sub = lax.axis_index("subset")
+    slab = lax.axis_index("slab")
     inside = (slice(None), pl.ds(8, rows), pl.ds(block, width))
     loads = [
         pltpu.make_async_copy(base_hbm, field_v.at[inside], load_sem.at[0]),
         pltpu.make_async_copy(z_hbm, own_v, load_sem.at[1]),
     ]
-    for load in loads:
+    smalls = [
+        pltpu.make_async_copy(delta_hbm, delta_ref, load_sem.at[2]),
+        pltpu.make_async_copy(pix_hbm, pix_ref, load_sem.at[3]),
+        pltpu.make_async_copy(w_hbm, w_ref, load_sem.at[4]),
+    ]
+    for load in smalls + loads:
         load.start()
+    for load in smalls:
+        load.wait()
     weights = [[[w_ref[a, b, c] for c in range(3)] for b in range(3)] for a in range(3)]
     share = -1.0 / sub_n
     sublanes = lax.broadcasted_iota(jnp.int32, (8, block), 0)
@@ -344,9 +351,9 @@
                 if place == 0:
                     patch(place, i, n, row + 8, col)
                 elif place == 1:
-                    pl.when(row == rows - 1)(functools.partial(patch, place, i, n, 7, col))
+                    pl.when((slab > 0) & (row == rows - 1))(functools.partial(patch, place, i, n, 7, col))
                 else:
-                    pl.when(row == 0)(functools.partial(patch, place, i, n, rows + 8, col))
+                    pl.when((slab < slab_n - 1) & (row == 0))(functools.partial(patch, place, i, n, rows + 8, col))
     stores = [pltpu.make_async_copy(field_v.at[inside], field_hbm, store_sem.at[0])]
     stores[0].start()
     for n in range(nblk):
@@ -384,8 +391,6 @@
     ray_blocks = measured.shape[2] // block
     inner, outer = split_group(slab_n)
     hbm = pl.BlockSpec(memory_space=pl.ANY)
-    vmem = pl.BlockSpec(memory_space=pltpu.VMEM)
-    smem = pl.BlockSpec(memory_space=pltpu.SMEM)
     dma = pltpu.SemaphoreType.DMA
     delta_shape = (3, sub_n, slices, nblk, block)
     pix_shape = (3, sub_n, 8, block)
@@ -397,8 +402,8 @@
             jax.ShapeDtypeStruct(pix_shape, jnp.int32),
             jax.ShapeDtypeStruct((slices, rows, width), jnp.float32),
         ),
-        in_specs=[pl.BlockSpec(memory_space=pltpu.HBM)] * 8,
-        out_specs=(vmem, vmem, hbm),
+        in_specs=[hbm] * 8,
+        out_specs=(hbm, hbm, hbm),
         scratch_shapes=[
             pltpu.VMEM(measured.shape, jnp.float32),
             pltpu.SMEM(ray_index.shape, jnp.int32),
@@ -412,10 +417,9 @@
             pltpu.VMEM((8, block), jnp.int32),
             pltpu.VMEM((inner, slices, ray_blocks, block), jnp.float32),
             pltpu.VMEM((outer, slices, ray_blocks, block), jnp.float32),
-            pltpu.VMEM(delta_shape, jnp.float32),
-            pltpu.VMEM(pix_shape, jnp.int32),
+            pltpu.VMEM((slices, nblk, block), jnp.float32),
             pltpu.VMEM(halo_shape, jnp.float32),
-            dma((8,)), dma,
+            dma((8,)), dma((3,)),
             dma((inner,)), dma((inner,)),
             dma((outer,)), dma((outer,)),
             dma((3, sub_n)), dma((3, sub_n)),
@@ -426,17 +430,20 @@
         name="rays",
     )(z_field, duals, tiles, measured, ray_index, pixel_index, step_size, kernel)
     return pl.pallas_call(
-        field_kernel,
+        functools.partial(field_kernel, slab_n),
         out_shape=(
             jax.ShapeDtypeStruct((slices, rows, width), jnp.float32),
             jax.ShapeDtypeStruct((1, slices, rows, width), jnp.float32),
         ),
-        in_specs=[hbm, hbm, vmem, smem, smem],
+        in_specs=[hbm] * 5,
         out_specs=(hbm, hbm),
         scratch_shapes=[
+            pltpu.VMEM(delta_shape, jnp.float32),
+            pltpu.SMEM(pix_shape, jnp.int32),
+            pltpu.SMEM(kernel.shape, jnp.float32),
             pltpu.VMEM((slices, rows + 16, width + 2 * block), jnp.float32),
             pltpu.VMEM((slices, rows, width), jnp.float32),
-            dma((2,)), dma((5,)),
+            dma((5,)), dma((5,)),
         ],
 
         name="field",

time: 22.2 us -> 19.6 us (0.88)
  Pallas kernels: 20.7 us -> 18.1 us
    pallas_call x1, Pallas kernels: 4.98 us -> 3.66 us  [body(): pl.pallas_call(functools.partial(field_kernel, slab_n), out_shape=(jax.Sh...]
    pallas_call x1, Pallas kernels: 15.7 us -> 14.5 us  [body(): pl.pallas_call(functools.partial(rays_kernel, sub_n, slab_n), out_shape=(...]
where the time goes in v3:
time: 19.6 us; the launch traced here: 19.4 us
  Pallas kernels  18.1 us (92%)
  between operations  1.29 us (7%)
    pallas_call x1, Pallas kernels, body(): pl.pallas_call(functools.partial(rays_kernel, sub_n, slab_n), out_shape=(...  14.5 us
    pallas_call x1, Pallas kernels, body(): pl.pallas_call(functools.partial(field_kernel, slab_n), out_shape=(jax.Sh...  3.66 us

profile of v3, /device:TPU:0, one launch (start us, length us, event | category | flops | bytes accessed | tf_op | source)
XLA Modules:
  0.0 19.4 jit_solution(4562628395290863440)
XLA Ops:
  1.3 14.5 %rays.1 = (f32[3,2,1,8,128]{4,3,2,1,0:T(8,128)}, s32[3,2,8,128]{3,2,1,0:T(8,128)}, f32[1,128,2048]{2,1,0:T(8,128)}) custom-call(f32[1,128,2048]{2,1,0:T(8,128)} %z_hbm.3, f32[1,1,128,2048]{3,2,1,0:T(8,128)} %dual_hbm.1, bf16[1,8,128,128]{3,2,1,0:T(8,128)(2,1)} %tile_hbm.1, f32[1,1,2048]{2,1,0:T(1,128)} %meas_hbm.1, s32[1,8]{1,0:T(1,128)} %ray_hbm.1, ...), custom_call_target="tpu_custom_call" | custom-call | tf_op jit(solution)/shard_map/rays/pallas_call | solution.py:398
  15.8 3.7 %field.1 = (f32[1,128,2048]{2,1,0:T(8,128)}, f32[1,1,128,2048]{3,2,1,0:T(8,128)}) custom-call(f32[1,128,2048]{2,1,0:T(8,128)} %z_hbm.3, f32[1,128,2048]{2,1,0:T(8,128)} %get-tuple-element.5.base_hbm, f32[3,2,1,8,128]{4,3,2,1,0:T(8,128)} %get-tuple-element.6.delta_hbm, s32[3,2,8,128]{3,2,1,0:T(8,128)} %get-tuple-element.7.pix_hbm, f32[3,3,3]{2,1,0:T(4,128)} %w_hbm.3), custom_call_target="tpu_custom_call" | custom-call | tf_op jit(solution)/shard_map/field/pallas_call | solution.py:432

commit v4 on v3

--- a/solution.py
+++ b/solution.py
@@ -8,7 +8,7 @@
 from jax.experimental.pallas import tpu as pltpu
 from jax.sharding import PartitionSpec as P
 
-
+GRANT = 16 * 1024 * 1024
 MESH = pl.DeviceIdType.MESH
 
 
@@ -395,6 +395,10 @@
     delta_shape = (3, sub_n, slices, nblk, block)
     pix_shape = (3, sub_n, 8, block)
     halo_shape = (2, slices, 1, width)
+    pinned = [
+        pltpu.with_memory_space_constraint(x, pltpu.HBM)
+        for x in (z_field, duals, tiles, measured, ray_index, pixel_index, kernel)
+    ]
     delta, pixels, base = pl.pallas_call(
         functools.partial(rays_kernel, sub_n, slab_n),
         out_shape=(
@@ -402,7 +406,7 @@
             jax.ShapeDtypeStruct(pix_shape, jnp.int32),
             jax.ShapeDtypeStruct((slices, rows, width), jnp.float32),
         ),
-        in_specs=[hbm] * 8,
+        in_specs=[pl.BlockSpec(memory_space=pltpu.HBM)] * 6 + [hbm, pl.BlockSpec(memory_space=pltpu.HBM)],
         out_specs=(hbm, hbm, hbm),
         scratch_shapes=[
             pltpu.VMEM(measured.shape, jnp.float32),
@@ -426,9 +430,9 @@
             dma((2, 1)), dma((2, 1)),
             dma((3, sub_n)), dma((3, sub_n)),
         ],
-        compiler_params=pltpu.CompilerParams(collective_id=0, has_side_effects=True),
+        compiler_params=pltpu.CompilerParams(collective_id=0, has_side_effects=True, vmem_limit_bytes=GRANT),
         name="rays",
-    )(z_field, duals, tiles, measured, ray_index, pixel_index, step_size, kernel)
+    )(*pinned[:6], step_size, pinned[6])
     return pl.pallas_call(
         functools.partial(field_kernel, slab_n),
         out_shape=(
@@ -446,6 +450,7 @@
             dma((5,)), dma((5,)),
         ],
 
+        compiler_params=pltpu.CompilerParams(vmem_limit_bytes=GRANT),
         name="field",
     )(z_field, base, delta, pixels, kernel)
 

time: 19.6 us -> 19 us (0.969)
  Pallas kernels: 18.1 us -> 17.5 us
    pallas_call x1, Pallas kernels: 3.66 us -> 3.16 us  [body(): pl.pallas_call(functools.partial(field_kernel, slab_n), out_shape=(jax.Sh...]
where the time goes in v4:
time: 19 us; the launch traced here: 18.8 us
  Pallas kernels  17.5 us (92%)
  between operations  1.32 us (7%)
    pallas_call x1, Pallas kernels, body(): pl.pallas_call(functools.partial(rays_kernel, sub_n, slab_n), out_shape=(...  14.4 us
    pallas_call x1, Pallas kernels, body(): pl.pallas_call(functools.partial(field_kernel, slab_n), out_shape=(jax.Sh...  3.16 us

profile of v4, /device:TPU:0, one launch (start us, length us, event | category | flops | bytes accessed | tf_op | source)
XLA Modules:
  0.0 18.8 jit_solution(9060229633944327515)
XLA Ops:
  1.3 0.0 copy-start
  1.3 0.0 copy-start.1
  1.3 14.4 %rays.1 = (f32[3,2,1,8,128]{4,3,2,1,0:T(8,128)S(1)}, s32[3,2,8,128]{3,2,1,0:T(8,128)S(1)}, f32[1,128,2048]{2,1,0:T(8,128)S(1)}) custom-call(f32[1,128,2048]{2,1,0:T(8,128)} %z_hbm.3, f32[1,1,128,2048]{3,2,1,0:T(8,128)} %dual_hbm.1, bf16[1,8,128,128]{3,2,1,0:T(8,128)(2,1)} %tile_hbm.1, f32[1,1,2048]{2,1,0:T(1,128)} %meas_hbm.1, s32[1,8]{1,0:T(1,128)} %ray_hbm.1, ...), custom_call_target="tpu_custom_call" | custom-call | tf_op jit(solution)/shard_map/rays/pallas_call | solution.py:402
  15.7 0.0 copy-done
  15.7 0.0 copy-done.1
  15.7 3.2 %field.1 = (f32[1,128,2048]{2,1,0:T(8,128)}, f32[1,1,128,2048]{3,2,1,0:T(8,128)}) custom-call(f32[1,128,2048]{2,1,0:T(8,128)S(1)} %copy-done, f32[1,128,2048]{2,1,0:T(8,128)S(1)} %get-tuple-element.5.base_hbm, f32[3,2,1,8,128]{4,3,2,1,0:T(8,128)S(1)} %get-tuple-element.6.delta_hbm, s32[3,2,8,128]{3,2,1,0:T(8,128)S(1)} %get-tuple-element.7.pix_hbm, ...), custom_call_target="tpu_custom_call" | custom-call | tf_op jit(solution)/shard_map/field/pallas_call | solution.py:436
Async XLA Ops:
  1.3 14.4 %copy-start = (f32[1,128,2048]{2,1,0:T(8,128)S(1)}, f32[1,128,2048]{2,1,0:T(8,128)}, u32[]{:S(2)}) copy-start(f32[1,128,2048]{2,1,0:T(8,128)} %z_hbm.3) | copy-start | bytes 3145732
  1.3 14.4 %copy-start.1 = (f32[3,3,3]{2,1,0:T(4,128)S(1)}, f32[3,3,3]{2,1,0:T(4,128)}, u32[]{:S(2)}) copy-start(f32[3,3,3]{2,1,0:T(4,128)} %w_hbm.3) | copy-start | bytes 328
